TPU v7x, 32 devices: a whole 2x2x4 slice. The times are simulated.
32 devices in a mesh: grp: 8 (over z, y), tm: 4 (over x, core).
Axes of the slice: x: 2, y: 2, z: 4, core: 2. Of those that a mesh axis runs over, the one named last changes fastest.
Arguments:
- voltages: bfloat16 [2, 192, 1048576], P(None, 'grp', 'tm'), may hold values from -6 to 6
- filter_taps: float32 [4, 4096], replicated, may hold values from -3 to 3
- delays: int32 [192, 1536], replicated, may hold values from 0 to 4095
- shifts: int32 [4, 512], replicated, may hold values from 0 to 2
Outputs:
- dedispersed: float32 [1536, 512, 32], P('grp', None, 'tm')
All inputs are finite; a program needn't handle non-finite values.
Results may differ from a plain program's by a relative error of at most 0.0014.
Values may be sent and summed in bfloat16 or wider, within the bound.
No kernel may reach another device: no remote copies, remote signals or barrier semaphores. Data moves between devices by JAX's collectives and lax.ppermute only.
A program may use at most 192 MiB of HBM per device.

v0:
```python
import math
import jax
import jax.numpy as jnp
from jax import lax
from jax.sharding import PartitionSpec as P

STATIONS = 192
TRANSFORM = 4096
CHANNELS = 512
TAPS = 4
INTEG = 8
LEVELS = 4
SHIFT_MOST = 2
two_pi = 2.0 * math.pi


def from_behind(x, axis, by):
    length = lax.axis_size(axis)
    pairs = [(i, i + by) for i in range(length) if 0 <= i + by < length]
    return lax.ppermute(x, axis, pairs)


def for_sending(x):
    return jax.tree.map(lambda a: a.astype(jnp.bfloat16) if a.dtype == jnp.float32 else a, x)


def dft_tables():
    rows_index = jnp.arange(CHANNELS, dtype=jnp.int32)
    cols_index = jnp.arange(TRANSFORM, dtype=jnp.int32)
    product = rows_index[:, None] * cols_index[None, :] % TRANSFORM
    angles = product.astype(jnp.float32) * (two_pi / TRANSFORM)
    scaling = 1.0 / math.sqrt(TRANSFORM)
    return (
        (jnp.cos(angles) * scaling).astype(jnp.bfloat16),
        (jnp.sin(angles) * scaling).astype(jnp.bfloat16),
    )


def beam_weights(channel, delays):
    phases = (channel * delays.T % TRANSFORM).astype(jnp.float32) * (two_pi / TRANSFORM)
    scaling = 1.0 / math.sqrt(STATIONS)
    return (
        (jnp.cos(phases) * scaling).astype(jnp.bfloat16),
        (jnp.sin(phases) * scaling).astype(jnp.bfloat16),
    )


def to_spectra(filtered, cosine, sine):
    real_part = jnp.einsum(
        "kn,stn->kst", cosine, filtered[0], preferred_element_type=jnp.float32
    ) + jnp.einsum("kn,stn->kst", sine, filtered[1], preferred_element_type=jnp.float32)
    imag_part = jnp.einsum(
        "kn,stn->kst", cosine, filtered[1], preferred_element_type=jnp.float32
    ) - jnp.einsum("kn,stn->kst", sine, filtered[0], preferred_element_type=jnp.float32)
    spectra = jnp.stack([real_part, imag_part]).astype(jnp.bfloat16)
    return spectra.reshape(2, CHANNELS, spectra.shape[2], -1, INTEG)


def dedisperse_level(leading, trailing, amounts, out_len):
    shifted = jnp.zeros(leading.shape[:3] + (2, out_len), jnp.float32)
    for offset in range(SHIFT_MOST + 1):
        selector = (amounts == offset).astype(jnp.float32)[None, :, :, :, None]
        shifted = shifted + selector * trailing[:, :, :, None, offset : offset + out_len]
    combined = 0.5 * (leading[:, :, :, None, :] + shifted)
    return combined.reshape(leading.shape[0], -1, out_len)


def local(voltages, filter_taps, delays, shifts):
    station_count = voltages.shape[1]
    frames = voltages.shape[2] // TRANSFORM
    framed = voltages.reshape(2, station_count, frames, TRANSFORM)
    last_frames = framed[:, :, frames - (TAPS - 1) :, :]
    previous = from_behind(last_frames, "tm", 1)
    extended = jnp.concatenate([previous, framed], axis=2).astype(jnp.float32)
    filtered = jnp.zeros((2, station_count, frames, TRANSFORM), jnp.float32)
    for tap in range(TAPS):
        start = TAPS - 1 - tap
        filtered = (
            filtered
            + filter_taps[tap][None, None, None, :] * extended[:, :, start : start + frames, :]
        )
    filtered = filtered.astype(jnp.bfloat16)
    cosine, sine = dft_tables()
    local_channels = CHANNELS // lax.axis_size("grp")
    spectra_all = to_spectra(filtered, cosine, sine)
    received = lax.all_to_all(spectra_all, "grp", split_axis=1, concat_axis=2, tiled=True)
    item_count = received.shape[3]
    all_stations = received.shape[2]
    spectra = received.reshape(2, local_channels, all_stations, item_count * INTEG)
    first_channel = lax.axis_index("grp") * local_channels

    def channel_powers(local_index):
        channel_data = lax.dynamic_index_in_dim(spectra, local_index, 1, keepdims=False)
        weight_cos, weight_sin = beam_weights(first_channel + local_index, delays)
        beam_real = jnp.dot(
            weight_cos, channel_data[0], preferred_element_type=jnp.float32
        ) + jnp.dot(weight_sin, channel_data[1], preferred_element_type=jnp.float32)
        beam_imag = jnp.dot(
            weight_cos, channel_data[1], preferred_element_type=jnp.float32
        ) - jnp.dot(weight_sin, channel_data[0], preferred_element_type=jnp.float32)
        energy = beam_real * beam_real + beam_imag * beam_imag
        power = energy.reshape(energy.shape[0], item_count, INTEG).sum(axis=-1) * (1.0 / INTEG)
        return power.astype(jnp.bfloat16)

    powers = lax.map(channel_powers, jnp.arange(local_channels, dtype=jnp.int32))
    powers = jnp.transpose(powers, (1, 0, 2))
    owned = lax.all_to_all(powers, "grp", split_axis=0, concat_axis=1, tiled=True)
    current = owned.astype(jnp.float32)
    beam_count = current.shape[0]
    power_len = current.shape[2]
    for level_index in range(1, LEVELS + 1):
        half_width = 2 ** (level_index - 1)
        group_count = CHANNELS // (2 * half_width)
        grouped = current.reshape(beam_count, group_count, 2, half_width, power_len)
        leading = grouped[:, :, 0]
        trailing_own = grouped[:, :, 1]
        next_rim = from_behind(for_sending(trailing_own[:, :, :, :SHIFT_MOST]), "tm", -1)
        trailing = jnp.concatenate([trailing_own, next_rim], axis=3)
        amounts = shifts[level_index - 1].reshape(group_count, half_width, 2)
        current = dedisperse_level(leading, trailing, amounts, power_len)
    return current


def solution(mesh):
    placed = (P(None, "grp", "tm"), P(), P(), P())
    return jax.shard_map(
        local, mesh=mesh, in_specs=placed, out_specs=P("grp", None, "tm"), check_vma=False
    )
```

profile of v0, /device:TPU:1, one launch (start us, length us, event | category | flops | bytes accessed | tf_op | source)
XLA Modules:
  0.0 1462.5 jit_solution(16832688132228220939)
XLA Ops:
  0.0 21.3 %copy.154 = bf16[6,8,64,4096]{3,2,1,0:T(8,128)(2,1)S(1)} copy(bf16[6,8,64,4096]{3,1,2,0:T(8,128)(2,1)} %bitcast.195) | data formatting | bytes 50331648
  27.7 13.1 collective-permute-done
  41.8 19.4 %maximum_convert_fusion = f32[2,24,67,4096]{3,2,1,0:T(8,128)} fusion(bf16[2,24,64,4096]{3,2,1,0:T(8,128)(2,1)S(1)} %bitcast.192, bf16[2,24,3,4096]{3,2,1,0:T(4,128)(2,1)S(1)} %copy.126), kind=kLoop, calls=%fused_computation.34 | loop fusion | flops 52690944 | bytes 79036416 | tf_op jit(solution)/shard_map/convert_element_type | solution.py:74
  61.1 76.4 %fusion.17 = bf16[2,24,64,4096]{3,2,1,0:T(8,128)(2,1)} fusion(f32[2,24,67,4096]{3,2,1,0:T(8,128)} %maximum_convert_fusion, f32[4096]{0:T(1024)S(1)} %bitcast.215, f32[4096]{0:T(1024)S(1)} %bitcast.216, f32[4096]{0:T(1024)S(1)} %bitcast.214, f32[4096]{0:T(1024)S(1)} %bitcast.213), kind=kLoop, calls=%fused_computation.28 | loop fusion | flops 100663296 | bytes 226557952 | tf_op jit(solution)/shard_map/convert_element_type | solution.py:82
  137.5 43.1 %fusion.23 = f32[512,24,64]{0,2,1:T(8,128)} fusion(bf16[2,24,64,4096]{3,2,1,0:T(8,128)(2,1)} %fusion.17), kind=kOutput, calls=%fused_computation.43 | convolution fusion | flops 6476005376 | bytes 15728640 | tf_op jit(solution)/shard_map/kn,stn->kst/dot_general | solution.py:51
  180.7 42.4 %fusion.20 = f32[512,24,64]{0,2,1:T(8,128)S(1)} fusion(bf16[2,24,64,4096]{3,2,1,0:T(8,128)(2,1)} %fusion.17), kind=kOutput, calls=%fused_computation.40 | convolution fusion | flops 6476005376 | bytes 15728640 | tf_op jit(solution)/shard_map/kn,stn->kst/dot_general | solution.py:54
  223.1 43.9 %fusion.48 = bf16[1,512,24,8,8]{1,4,3,2,0:T(8,128)(2,1)S(1)} fusion(f32[512,24,64]{0,2,1:T(8,128)} %fusion.23, bf16[2,24,64,4096]{3,2,1,0:T(8,128)(2,1)} %fusion.17), kind=kOutput, calls=%fused_computation.89 | convolution fusion | flops 6477578240 | bytes 17301504 | tf_op jit(solution)/shard_map/kn,stn->kst/dot_general | solution.py:49
  266.9 41.9 %fusion.51 = bf16[1,512,24,8,8]{1,4,3,2,0:T(8,128)(2,1)S(1)} fusion(f32[512,24,64]{0,2,1:T(8,128)S(1)} %fusion.20, bf16[2,24,64,4096]{3,2,1,0:T(8,128)(2,1)} %fusion.17), kind=kOutput, calls=%fused_computation.90 | convolution fusion | flops 6477578240 | bytes 17301504 | tf_op jit(solution)/shard_map/kn,stn->kst/dot_general | solution.py:52
  309.1 26.3 %copy.127 = bf16[2,512,24,8,8]{2,4,3,0,1:T(8,128)(2,1)} copy(bf16[2,512,24,8,8]{1,4,3,2,0:T(8,128)(2,1)S(1)} %pad_maximum_fusion) | data formatting | bytes 6291456 | tf_op jit(solution)/shard_map/stack | solution.py:55
  335.5 24.2 %reshape.336 = bf16[8,2,98304]{2,1,0:T(2,128)(2,1)} reshape(bf16[512,2,8,8,24]{4,3,2,1,0:T(8,128)(2,1)} %bitcast.193) | data formatting | bytes 6291456
  359.7 5.8 all-to-all-start
  365.5 60.2 %all-to-all-done = bf16[8,2,98304]{2,1,0:T(2,128)(2,1)S(1)} async-done(((bf16[8,2,98304]{2,1,0:T(2,128)(2,1)}), bf16[8,2,98304]{2,1,0:T(2,128)(2,1)S(1)}, u32[]{:S(2)}, u32[]{:S(2)}) %all-to-all-start) | async-done | bytes 3145760 | tf_op jit(solution)/shard_map/all_to_all | solution.py:86
  425.8 25.3 %reshape.337 = bf16[512,2,8,8,24]{4,3,2,1,0:T(8,128)(2,1)} reshape(bf16[8,2,98304]{2,1,0:T(2,128)(2,1)S(1)} %all-to-all-done) | data formatting | bytes 6291456
  451.1 25.2 %copy.129 = bf16[2,64,8,24,8,8]{1,5,4,3,2,0:T(8,128)(2,1)} copy(bf16[2,64,8,24,8,8]{3,5,4,0,1,2:T(8,128)(2,1)} %bitcast.194) | data formatting | bytes 6291456 | tf_op jit(solution)/shard_map/all_to_all | solution.py:86
  476.3 9.6 copy.130
  485.9 832.3 %while.12 = (s32[]{:T(128)}, bf16[64,1536,8]{1,2,0:T(8,128)(2,1)}, s32[64]{0:T(128)S(1)}, s32[]{:T(128)}, s32[192,1536]{1,0:T(8,128)S(1)}, /*index=5*/bf16[2,64,...) while((s32[]{:T(128)}, bf16[64,1536,8]{1,2,0:T(8,128)(2,1)}, s32[64]{0:T(128)S(1)}, s32[]{:T(128)}, ...), condition=%wide.region_2.3_spmd, body=%wide.region_0.2_spmd.sunk | while | flops 156905472 | bytes 7398087 | solution.py:105
  541.1 4.8 multiply_convert_fusion.6
  567.1 4.8 multiply_convert_fusion.6
  1324.5 5.8 reshape.338
  1330.3 38.8 %all_to_all.24 = bf16[8,2,49152]{2,1,0:T(2,128)(2,1)} all-to-all(bf16[8,2,49152]{2,1,0:T(2,128)(2,1)S(1)} %reshape.338), channel_id=1, replica_groups=mesh['grp'=8,'tm'=4] {'grp'}, dimensions={0} | all-to-all | bytes 3145728 | tf_op jit(solution)/shard_map/all_to_all | solution.py:107
  1369.1 5.2 reshape.339
  1432.3 5.4 collective-permute-done.3
  1446.8 5.1 collective-permute-done.4
  1456.8 5.2 copy.148
  (532 shorter events, 740.0 us)
Async XLA Ops:
  21.3 6.4 copy-start.6
  23.1 17.6 %collective-permute-start = (bf16[2,24,3,4096]{3,1,2,0:T(8,128)(2,1)S(1)}, bf16[2,24,3,4096]{3,1,2,0:T(8,128)(2,1)S(1)}, u32[]{:S(2)}, u32[]{:S(2)}) collective-permute-start(bf16[2,24,3,4096]{3,1,2,0:T(8,128)(2,1)S(1)} %copy.125), channel_id=1, source_target_pairs={{0,1},{1,2},{2,3},{4,5},{5,6},{6,7},{8,9},{9,10},{10,11},{12,13},{... | collective-permute-start | bytes 3538952 | tf_op jit(solution)/shard_map/ppermute | solution.py:20
  359.7 66.0 %all-to-all-start = ((bf16[8,2,98304]{2,1,0:T(2,128)(2,1)}), bf16[8,2,98304]{2,1,0:T(2,128)(2,1)S(1)}, u32[]{:S(2)}, u32[]{:S(2)}) async-start(bf16[8,2,98304]{2,1,0:T(2,128)(2,1)} %reshape.336), calls=%async_computation | async-start | bytes 6291456 | tf_op jit(solution)/shard_map/all_to_all | solution.py:86
  476.3 9.6 copy-start
  1378.3 8.6 copy-start.7
  1385.0 8.0 collective-permute-start.1
  1390.0 3.0 copy-start.5
  1406.6 7.1 collective-permute-start.2
  1421.9 1.6 copy-start.3
  1422.3 1.9 copy-start.2
  1423.9 1.7 copy-start.1
  1430.0 7.7 collective-permute-start.3
  1439.2 1.6 copy-start.4
  1444.2 7.7 collective-permute-start.4
where the time goes:
time: 1480 us; the launch traced here: 1460 us
  other arithmetic  464 us (31%)
  matrix products  449 us (30%)
  local copies, waits for them, and re-layouts  238 us (16%)
  loops' own time  168 us (11%)
  waiting for transfers between devices  84.6 us (6%)
  blocking collectives  38.8 us (3%)
  starting transfers between devices  18 us (1%)
    convert_element_type x64, other arithmetic, beam_weights(): (jnp.sin(phases) * scaling).astype(jnp.bfloat16)  309 us
    another operation x1, loops' own time, local(): lax.map(channel_powers, jnp.arange(local_channels, dtype=jnp.int32))  168 us
    unnamed x23, local copies, waits for them, and re-layouts  89.1 us
    convert_element_type x1, other arithmetic, local(): filtered = filtered.astype(jnp.bfloat16)  76.4 us
    dot_general x64, matrix products, channel_powers(): jnp.dot(weight_sin, channel_data[0], preferred_element_type=jnp.float32)  73 us
    dot_general x64, matrix products, channel_powers(): jnp.dot(weight_sin, channel_data[1], preferred_element_type=jnp.float32)  68.7 us
    dot_general x64, matrix products, channel_powers(): jnp.dot(weight_cos, channel_data[1], preferred_element_type=jnp.float32)  68.3 us
    dot_general x64, matrix products, channel_powers(): jnp.dot(weight_cos, channel_data[0], preferred_element_type=jnp.float32)  68.2 us
  transfers between devices with their start and end apart: 6, of which 5 were waited for; matrix products, arithmetic and copies ran while one was open for 1% of the time, Pallas kernels for 0%

commit v1 on v0

--- a/solution.py
+++ b/solution.py
@@ -83,7 +83,12 @@
     cosine, sine = dft_tables()
     local_channels = CHANNELS // lax.axis_size("grp")
     spectra_all = to_spectra(filtered, cosine, sine)
-    received = lax.all_to_all(spectra_all, "grp", split_axis=1, concat_axis=2, tiled=True)
+    received = jnp.concatenate(
+        lax.all_to_all(
+            jnp.stack(jnp.split(spectra_all, lax.axis_size("grp"), axis=1)), "grp", 0, 0
+        ),
+        axis=2,
+    )
     item_count = received.shape[3]
     all_stations = received.shape[2]
     spectra = received.reshape(2, local_channels, all_stations, item_count * INTEG)

time: 1480 us -> 1410 us (0.953)
  local copies, waits for them, and re-layouts: 238 us -> 163 us
    unnamed x23, local copies, waits for them, and re-layouts: 89.1 us -> 57.3 us
    another operation x1 -> x0, local copies, waits for them, and re-layouts: 26.3 us -> none  [to_spectra(): spectra = jnp.stack([real_part, imag_part]).astype(jnp.bfloat16)]
    all_to_all x1 -> x0, local copies, waits for them, and re-layouts: 25.2 us -> none  [local(): lax.all_to_all(spectra_all, 'grp', split_axis=1, concat_axis=2, tiled=True)]
where the time goes in v1:
time: 1410 us; the launch traced here: 1390 us
  other arithmetic  469 us (33%)
  matrix products  449 us (32%)
  loops' own time  168 us (12%)
  local copies, waits for them, and re-layouts  163 us (12%)
  waiting for transfers between devices  84.6 us (6%)
  blocking collectives  38.8 us (3%)
  starting transfers between devices  17.7 us (1%)
    convert_element_type x64, other arithmetic, beam_weights(): (jnp.sin(phases) * scaling).astype(jnp.bfloat16)  309 us
    another operation x1, loops' own time, local(): lax.map(channel_powers, jnp.arange(local_channels, dtype=jnp.int32))  168 us
    convert_element_type x1, other arithmetic, local(): filtered = filtered.astype(jnp.bfloat16)  76.4 us
    dot_general x64, matrix products, channel_powers(): jnp.dot(weight_sin, channel_data[0], preferred_element_type=jnp.float32)  73 us
    dot_general x64, matrix products, channel_powers(): jnp.dot(weight_sin, channel_data[1], preferred_element_type=jnp.float32)  68.7 us
    dot_general x64, matrix products, channel_powers(): jnp.dot(weight_cos, channel_data[1], preferred_element_type=jnp.float32)  68.3 us
    dot_general x64, matrix products, channel_powers(): jnp.dot(weight_cos, channel_data[0], preferred_element_type=jnp.float32)  68.2 us
    all_to_all x1, waiting for transfers between devices, local(): lax.all_to_all(jnp.stack(jnp.split(spectra_all, lax.axis_size('grp'), axi...  60.3 us
  transfers between devices with their start and end apart: 6, of which 5 were waited for; matrix products, arithmetic and copies ran while one was open for 1% of the time, Pallas kernels for 0%

profile of v1, /device:TPU:1, one launch (start us, length us, event | category | flops | bytes accessed | tf_op | source)
XLA Modules:
  0.0 1391.4 jit_solution(970233014241460200)
XLA Ops:
  0.0 21.3 %copy.153 = bf16[6,8,64,4096]{3,2,1,0:T(8,128)(2,1)S(1)} copy(bf16[6,8,64,4096]{3,1,2,0:T(8,128)(2,1)} %bitcast.224) | data formatting | bytes 50331648
  27.7 13.1 collective-permute-done
  41.8 19.4 %maximum_convert_fusion = f32[2,24,67,4096]{3,2,1,0:T(8,128)} fusion(bf16[2,24,64,4096]{3,2,1,0:T(8,128)(2,1)S(1)} %bitcast.223, bf16[2,24,3,4096]{3,2,1,0:T(4,128)(2,1)S(1)} %copy.129), kind=kLoop, calls=%fused_computation.34 | loop fusion | flops 52690944 | bytes 79036416 | tf_op jit(solution)/shard_map/convert_element_type | solution.py:74
  61.1 76.4 %fusion.17 = bf16[2,24,64,4096]{3,2,1,0:T(8,128)(2,1)} fusion(f32[2,24,67,4096]{3,2,1,0:T(8,128)} %maximum_convert_fusion, f32[4096]{0:T(1024)S(1)} %bitcast.245, f32[4096]{0:T(1024)S(1)} %bitcast.246, f32[4096]{0:T(1024)S(1)} %bitcast.244, f32[4096]{0:T(1024)S(1)} %bitcast.243), kind=kLoop, calls=%fused_computation.28 | loop fusion | flops 100663296 | bytes 226557952 | tf_op jit(solution)/shard_map/convert_element_type | solution.py:82
  137.5 43.1 %fusion.20 = f32[512,24,64]{0,2,1:T(8,128)} fusion(bf16[2,24,64,4096]{3,2,1,0:T(8,128)(2,1)} %fusion.17), kind=kOutput, calls=%fused_computation.40 | convolution fusion | flops 6476005376 | bytes 15728640 | tf_op jit(solution)/shard_map/kn,stn->kst/dot_general | solution.py:54
  180.7 42.4 %fusion.23 = f32[512,24,64]{0,2,1:T(8,128)S(1)} fusion(bf16[2,24,64,4096]{3,2,1,0:T(8,128)(2,1)} %fusion.17), kind=kOutput, calls=%fused_computation.43 | convolution fusion | flops 6476005376 | bytes 15728640 | tf_op jit(solution)/shard_map/kn,stn->kst/dot_general | solution.py:51
  223.1 43.9 %fusion.51 = bf16[1,512,24,8,8]{1,4,3,2,0:T(8,128)(2,1)S(1)} fusion(f32[512,24,64]{0,2,1:T(8,128)} %fusion.20, bf16[2,24,64,4096]{3,2,1,0:T(8,128)(2,1)} %fusion.17), kind=kOutput, calls=%fused_computation.103 | convolution fusion | flops 6477578240 | bytes 17301504 | tf_op jit(solution)/shard_map/kn,stn->kst/dot_general | solution.py:52
  266.9 41.9 %fusion.48 = bf16[1,512,24,8,8]{1,4,3,2,0:T(8,128)(2,1)S(1)} fusion(f32[512,24,64]{0,2,1:T(8,128)S(1)} %fusion.23, bf16[2,24,64,4096]{3,2,1,0:T(8,128)(2,1)} %fusion.17), kind=kOutput, calls=%fused_computation.102 | convolution fusion | flops 6477578240 | bytes 17301504 | tf_op jit(solution)/shard_map/kn,stn->kst/dot_general | solution.py:49
  314.4 8.9 reshape.335
  323.3 5.5 all-to-all-start
  328.9 60.3 %all-to-all-done = bf16[8,2,98304]{2,1,0:T(2,128)(2,1)S(1)} async-done(((bf16[8,2,98304]{2,1,0:T(2,128)(2,1)}), bf16[8,2,98304]{2,1,0:T(2,128)(2,1)S(1)}, u32[]{:S(2)}, u32[]{:S(2)}) %all-to-all-start) | async-done | bytes 3145760 | tf_op jit(solution)/shard_map/all_to_all | solution.py:87
  389.2 6.2 reshape.336
  403.8 9.6 copy.131
  413.4 832.4 %while.12 = (s32[]{:T(128)}, bf16[64,1536,8]{1,2,0:T(8,128)(2,1)}, s32[64]{0:T(128)S(1)}, s32[]{:T(128)}, s32[192,1536]{1,0:T(8,128)S(1)}, /*index=5*/bf16[2,64,...) while((s32[]{:T(128)}, bf16[64,1536,8]{1,2,0:T(8,128)(2,1)}, s32[64]{0:T(128)S(1)}, s32[]{:T(128)}, ...), condition=%wide.region_2.3_spmd, body=%wide.region_0.2_spmd.sunk | while | flops 156905472 | bytes 7398087 | solution.py:110
  416.6 4.8 multiply_convert_fusion.6
  429.6 4.8 multiply_convert_fusion.6
  585.7 4.8 multiply_convert_fusion.6
  598.7 4.8 multiply_convert_fusion.6
  1252.1 5.8 reshape.337
  1257.9 38.8 %all_to_all.14 = bf16[8,2,49152]{2,1,0:T(2,128)(2,1)} all-to-all(bf16[8,2,49152]{2,1,0:T(2,128)(2,1)S(1)} %reshape.337), channel_id=1, replica_groups=mesh['grp'=8,'tm'=4] {'grp'}, dimensions={0} | all-to-all | bytes 3145728 | tf_op jit(solution)/shard_map/all_to_all | solution.py:112
  1296.7 5.2 reshape.338
  1361.4 5.4 collective-permute-done.3
  1375.9 5.1 collective-permute-done.4
  1386.0 5.2 copy.149
  (539 shorter events, 745.6 us)
Async XLA Ops:
  21.3 6.4 copy-start.6
  23.1 17.6 %collective-permute-start = (bf16[2,24,3,4096]{3,1,2,0:T(8,128)(2,1)S(1)}, bf16[2,24,3,4096]{3,1,2,0:T(8,128)(2,1)S(1)}, u32[]{:S(2)}, u32[]{:S(2)}) collective-permute-start(bf16[2,24,3,4096]{3,1,2,0:T(8,128)(2,1)S(1)} %copy.128), channel_id=1, source_target_pairs={{0,1},{1,2},{2,3},{4,5},{5,6},{6,7},{8,9},{9,10},{10,11},{12,13},{... | collective-permute-start | bytes 3538952 | tf_op jit(solution)/shard_map/ppermute | solution.py:20
  311.8 2.7 copy-start.5
  323.3 65.8 %all-to-all-start = ((bf16[8,2,98304]{2,1,0:T(2,128)(2,1)}), bf16[8,2,98304]{2,1,0:T(2,128)(2,1)S(1)}, u32[]{:S(2)}, u32[]{:S(2)}) async-start(bf16[8,2,98304]{2,1,0:T(2,128)(2,1)} %reshape.335), calls=%async_computation | async-start | bytes 6291456 | tf_op jit(solution)/shard_map/all_to_all | solution.py:87
  403.8 9.6 copy-start
  1305.9 8.6 copy-start.7
  1312.5 7.8 collective-permute-start.1
  1335.7 7.1 collective-permute-start.2
  1351.0 1.6 copy-start.3
  1351.4 1.9 copy-start.2
  1353.0 1.7 copy-start.1
  1359.1 7.7 collective-permute-start.3
  1368.3 1.6 copy-start.4
  1373.3 7.7 collective-permute-start.4
